TPU v7x, 512 devices: a whole 4x8x8 slice. The times are simulated.
512 devices in a mesh: wide: 32 (over x, y), grp: 16 (over z, core).
Axes of the slice: x: 4, y: 8, z: 8, core: 2. Of those that a mesh axis runs over, the one named last changes fastest.
Arguments:
- amplitudes: bfloat16 [128, 128, 256, 256], P(None, 'wide', 'grp'), may hold values from -6 to 6
- integrals: bfloat16 [4, 128, 256, 256], P(None, 'grp', 'wide'), may hold values from -0.0625 to 0.0625
- pair_local: int32 [4, 128], replicated, may hold values from 0 to 1, as said below
Outputs:
- cycle_term: bfloat16 [4, 128, 256, 256], P(None, 'wide', 'grp')
Inputs may be any that keep to these rules, and one draw needn't show every extreme that they name: `pair_local`: 1 marks a pair (i, k) of occupied orbitals inside the locality domain, 0 a screened pair.
All inputs are finite; a program needn't handle non-finite values.
Results may differ from a plain program's by a relative error of at most 0.001.
Values may be sent and summed in bfloat16 or wider, within the bound.
No kernel may reach another device: no remote copies, remote signals or barrier semaphores. Data moves between devices by JAX's collectives and lax.ppermute only.
A program may use at most 128 MiB of HBM per device.

v0:
```python
import jax
import jax.numpy as jnp
from jax import lax
from jax.sharding import PartitionSpec as P


def body(amplitudes, integrals, pair_local):
    kept_rows = integrals.shape[1]
    operand = lax.all_to_all(amplitudes, "grp", split_axis=0, concat_axis=2, tiled=True)
    offset = lax.axis_index("grp") * kept_rows
    weights = lax.dynamic_slice_in_dim(pair_local, offset, kept_rows, 1)
    factor = weights.astype(jnp.bfloat16)[:, :, None, None]
    masked = lax.all_gather(integrals, "wide", axis=2, tiled=True) * factor
    partial_cycle = jnp.einsum(
        "ikac,kjcb->ijab", masked, operand, preferred_element_type=jnp.float32
    )
    summed = lax.psum_scatter(partial_cycle, "grp", scatter_dimension=2, tiled=True)
    return summed.astype(jnp.bfloat16)


def solution(mesh):
    in_specs = (P(None, "wide", "grp", None), P(None, "grp", "wide", None), P())
    out_specs = P(None, "wide", "grp", None)
    return jax.shard_map(body, mesh=mesh, in_specs=in_specs, out_specs=out_specs, check_vma=False)
```

profile of v0, /device:TPU:1, one launch (start us, length us, event | category | flops | bytes accessed | tf_op | source)
XLA Modules:
  0.0 198.8 jit_solution(1778886672320362762)
XLA Ops:
  6.5 0.0 all-gather.2.cloned.1.call-start
  6.5 0.7 all-gather.2.cloned.1.call-update
  7.3 0.0 copy-start
  7.3 11.8 %all-to-all-start = ((bf16[128,4,16,256]{3,2,1,0:T(8,128)(2,1)}), bf16[128,4,16,256]{3,2,1,0:T(8,128)(2,1)}, u32[]{:S(2)}, u32[]{:S(2)}) async-start(bf16[128,4,16,256]{3,2,1,0:T(8,128)(2,1)} %param.3), calls=%async_computation | async-start | bytes 8388608 | tf_op jit(solution)/shard_map/all_to_all | solution.py:9
  19.1 0.0 reduce-scatter.2.cloned.1.call-start
  19.1 0.0 copy-done
  19.2 0.1 dynamic-slice_convert_fusion
  19.2 93.4 %all-to-all-done = bf16[128,4,16,256]{3,2,1,0:T(8,128)(2,1)} async-done(((bf16[128,4,16,256]{3,2,1,0:T(8,128)(2,1)}), bf16[128,4,16,256]{3,2,1,0:T(8,128)(2,1)}, u32[]{:S(2)}, u32[]{:S(2)}) %all-to-all-start) | async-done | bytes 4194336 | tf_op jit(solution)/shard_map/all_to_all | solution.py:9
  112.6 4.7 %copy.4 = bf16[16,8,4,16,256]{4,3,0,1,2:T(8,128)(2,1)} copy(bf16[16,8,4,16,256]{4,3,2,1,0:T(8,128)(2,1)} %bitcast.2) | data formatting | bytes 8388608 | tf_op jit(solution)/shard_map/all_to_all | solution.py:9
  117.3 0.0 all-gather.2.cloned.1.call-done
  117.3 10.0 %fusion.3 = f32[4,4,256,256]{3,2,1,0:T(8,128)} fusion(bf16[8,4,256,256,1]{3,2,0,1,4:T(8,128)(2,1)} %bitcast.19, bf16[4,8,256,256]{3,2,1,0:T(8,128)(2,1)} %all-gather.2.cloned.1.call-done, bf16[4,8]{1,0:T(4,128)(2,1)S(1)} %dynamic-slice_convert_fusion), kind=kOutput, calls=%fused_computation.3 | convolution fusion | flops 4303355904 | bytes 12582976 | tf_op jit(solution)/shard_map/ikac,kjcb->ijab/dot_general | solution.py:14
  127.3 0.0 reduce-scatter.2.cloned.1.call-update
  127.3 63.0 %reduce-scatter.2.cloned.1.call-done = f32[4,4,16,256]{3,2,1,0:T(8,128)} async-done(((f32[4,4,256,256]{3,2,1,0:T(8,128)}), f32[4,4,16,256]{3,2,1,0:T(8,128)}) %reduce-scatter.2.cloned.1.call-update) | async-done | bytes 262160 | tf_op jit(solution)/shard_map/reduce_scatter | solution.py:17
  190.4 1.6 convert_element_type.7
Async XLA Ops:
  6.5 110.8 %all-gather.2.cloned.1.call-start = ((), (), s32[]{:S(2)}) async-start(), calls=%async_computation.2 | async-start | bytes 4325376 | tf_op jit(solution)/shard_map/all_gather | solution.py:13
  7.3 11.9 %copy-start = (s32[4,128]{1,0:T(4,128)S(1)}, s32[4,128]{1,0:T(4,128)}, u32[]{:S(2)}) copy-start(s32[4,128]{1,0:T(4,128)} %param.5) | copy-start | bytes 6148
  7.3 105.3 %all-to-all-start = ((bf16[128,4,16,256]{3,2,1,0:T(8,128)(2,1)}), bf16[128,4,16,256]{3,2,1,0:T(8,128)(2,1)}, u32[]{:S(2)}, u32[]{:S(2)}) async-start(bf16[128,4,16,256]{3,2,1,0:T(8,128)(2,1)} %param.3), calls=%async_computation | async-start | bytes 8388608 | tf_op jit(solution)/shard_map/all_to_all | solution.py:9
  19.1 171.3 %reduce-scatter.2.cloned.1.call-start = ((), (), s32[]{:S(2)}) async-start(), calls=%async_computation.3 | async-start | bytes 4456448 | tf_op jit(solution)/shard_map/reduce_scatter | solution.py:17
Sparse Core Ops, SparseCore 0:
  10.4 90.4 all-gather.1
  127.4 62.8 reduce-scatter.1
where the time goes:
time: 201 us; the launch traced here: 199 us
  waiting for transfers between devices  157 us (78%)
  between operations  13.4 us (7%)
  starting transfers between devices  11.9 us (6%)
  matrix products  9.95 us (5%)
  local copies, waits for them, and re-layouts  4.72 us (2%)
    all_to_all x1, waiting for transfers between devices, body(): lax.all_to_all(amplitudes, 'grp', split_axis=0, concat_axis=2, tiled=True)  93.4 us
    reduce_scatter x1, waiting for transfers between devices, body(): lax.psum_scatter(partial_cycle, 'grp', scatter_dimension=2, tiled=True)  63 us
    all_to_all x1, starting transfers between devices, body(): lax.all_to_all(amplitudes, 'grp', split_axis=0, concat_axis=2, tiled=True)  11.8 us
    dot_general x1, matrix products, body(): jnp.einsum('ikac,kjcb->ijab', masked, operand, preferred_element_type=jnp...  9.95 us
    all_to_all x1, local copies, waits for them, and re-layouts, body(): lax.all_to_all(amplitudes, 'grp', split_axis=0, concat_axis=2, tiled=True)  4.72 us
  transfers between devices with their start and end apart: 3, of which 2 were waited for; matrix products, arithmetic and copies ran while one was open for 2% of the time, Pallas kernels for 0%

commit v1 on v0

v1 whole, which is shorter than its diff:
```python
import jax
import jax.numpy as jnp
from jax import lax
from jax.experimental import pallas as pl
from jax.experimental.pallas import tpu as pltpu
from jax.sharding import Mesh, PartitionSpec as P

BF16, F16, F32 = jnp.bfloat16, jnp.float16, jnp.float32
LADDER = (64, 32, 16, 8, 4, 2, 1)


def raise_to_range(peak):
    peak = jnp.maximum(peak, 2.0**-100)
    scale, power = jnp.ones_like(peak), jnp.zeros_like(peak)
    for step in LADDER:
        fits = peak * scale <= 2.0 ** (15 - step)
        scale = jnp.where(fits, scale * 2.0**step, scale)
        power = jnp.where(fits, power + step, power)
    return scale, power


def lower_again(power):
    scale, left = jnp.ones_like(power), power
    for step in LADDER:
        take = left >= step
        scale = jnp.where(take, scale * 2.0**-step, scale)
        left = jnp.where(take, left - step, left)
    return scale


def product_kernel(inverse_ref, w_ref, t_ref, out_ref):
    pair = pl.program_id(1)
    rows = jnp.concatenate(
        [w_ref[:, :, g].reshape(256, 128) for g in range(16)], axis=1
    )
    columns = t_ref[:, 0].reshape(2048, 256)
    acc = jnp.dot(rows, columns, preferred_element_type=F32).reshape(2, 4, 32, 256)
    for half in range(2):
        out_ref[0, :, 0, half] = acc[half] * inverse_ref[2 * pair + half]


def product(inverse, w, t):
    return pl.pallas_call(
        product_kernel,
        grid_spec=pltpu.PrefetchScalarGridSpec(
            num_scalar_prefetch=1,
            grid=(4, 4),
            in_specs=[
                pl.BlockSpec((2, 4, 16, 32, 128), lambda j, m, s: (m, 0, 0, 0, 0)),
                pl.BlockSpec((128, 1, 16, 256), lambda j, m, s: (0, j, 0, 0)),
            ],
            out_specs=pl.BlockSpec(
                (1, 4, 1, 2, 32, 256), lambda j, m, s: (m % 2, 0, m // 2, 0, 0, j)
            ),
        ),
        out_shape=jax.ShapeDtypeStruct((2, 4, 2, 2, 32, 1024), F32),
        cost_estimate=pl.CostEstimate(
            flops=2 * 1024 * 2048 * 1024, bytes_accessed=12 << 20, transcendentals=0
        ),
    )(inverse, w, t)


def body(amplitudes, integrals, pair_local):
    group = lax.axis_index(("z", "core"))
    weights = lax.dynamic_slice_in_dim(pair_local, group * 8, 8, 1)
    masked = integrals * weights.astype(BF16)[:, :, None, None]
    pieces = masked.reshape(4, 8, 8, 16, 16).transpose(3, 0, 2, 1, 4).reshape(16, 32, 128)
    pieces = jnp.broadcast_to(pieces[None], (4, 16, 32, 128)).reshape(64, 32, 128)
    block = lax.all_to_all(pieces, ("x", "z", "core"), 0, 0, tiled=True)
    block = block.reshape(2048, 128).astype(F32)
    scale, power = raise_to_range(jnp.max(jnp.abs(block)))
    sent = jnp.concatenate(
        [(block * scale).astype(F16), jnp.broadcast_to(power.astype(F16), (16, 128))]
    )
    gathered = lax.all_gather(sent, "y", axis=0)
    inverse = lower_again(gathered[:, 2048, 0].astype(F32))
    w = gathered[:, :2048].astype(BF16).reshape(8, 4, 16, 32, 128)
    part = product(inverse, w, amplitudes).reshape(2, 512, 1024)
    both = lax.all_to_all(part, "core", 0, 0, tiled=True)
    chip = (both[0] + both[1]).reshape(8, 64, 1024)
    shares = lax.all_to_all(chip, "z", 0, 0, tiled=True)
    total = jnp.sum(shares, axis=0).astype(BF16)
    total = total.reshape(2, 4, 8, 4, 256).transpose(1, 3, 0, 2, 4)
    return total.reshape(4, 4, 16, 256)


def solution(mesh):
    chips = Mesh(mesh.devices.reshape(4, 8, 8, 2), ("x", "y", "z", "core"))
    wide, grp = ("x", "y"), ("z", "core")
    in_specs = (P(None, wide, grp, None), P(None, grp, wide, None), P())
    out_specs = P(None, wide, grp, None)
    return jax.shard_map(body, mesh=chips, in_specs=in_specs, out_specs=out_specs, check_vma=False)
```

time: 201 us -> 169 us (0.84)
  waiting for transfers between devices: 157 us -> 0 us
  blocking collectives: 0 us -> 140 us
  Pallas kernels: 0 us -> 17.9 us
  between operations: 13.4 us -> 0.78 us
  starting transfers between devices: 11.9 us -> 0 us
  matrix products: 9.95 us -> 0 us
  other arithmetic: 1.7 us -> 6.65 us
    all_to_all x0 -> x3, blocking collectives: none -> 95.3 us  [the longest x1 54.2 us: body(): shares = lax.all_to_all(chip, 'z', 0, 0, tiled=True)]
    all_to_all x1 -> x0, waiting for transfers between devices: 93.4 us -> none  [body(): lax.all_to_all(amplitudes, 'grp', split_axis=0, concat_axis=2, tiled=True)]
    reduce_scatter x1 -> x0, waiting for transfers between devices: 63 us -> none  [body(): lax.psum_scatter(partial_cycle, 'grp', scatter_dimension=2, tiled=True)]
    all_gather x0 -> x1, blocking collectives: none -> 45.1 us  [body(): gathered = lax.all_gather(sent, 'y', axis=0)]
    pallas_call x0 -> x1, Pallas kernels: none -> 17.9 us  [product(): pl.pallas_call(product_kernel, grid_spec=pltpu.PrefetchScalarGridSpec(num...]
    all_to_all x1 -> x0, starting transfers between devices: 11.8 us -> none  [body(): lax.all_to_all(amplitudes, 'grp', split_axis=0, concat_axis=2, tiled=True)]
    dot_general x1 -> x0, matrix products: 9.95 us -> none  [body(): jnp.einsum('ikac,kjcb->ijab', masked, operand, preferred_element_type=jnp...]
    all_to_all x1 -> x0, local copies, waits for them, and re-layouts: 4.72 us -> none  [body(): lax.all_to_all(amplitudes, 'grp', split_axis=0, concat_axis=2, tiled=True)]
  transfers between devices with their start and end apart: 3 -> 0, of which waited for: 2 -> 0; matrix products, arithmetic and copies ran while one was open for 2% -> 0% of each run, Pallas kernels for 0% -> 0%
where the time goes in v1:
time: 169 us
  blocking collectives  140 us (83%)
  Pallas kernels  17.9 us (11%)
  other arithmetic  6.65 us (4%)
  local copies, waits for them, and re-layouts  2.99 us (2%)
    all_to_all x1, blocking collectives, body(): shares = lax.all_to_all(chip, 'z', 0, 0, tiled=True)  54.2 us
    all_gather x1, blocking collectives, body(): gathered = lax.all_gather(sent, 'y', axis=0)  45.1 us
    all_to_all x1, blocking collectives, body(): block = lax.all_to_all(pieces, ('x', 'z', 'core'), 0, 0, tiled=True)  31.9 us
    pallas_call x1, Pallas kernels, product(): pl.pallas_call(product_kernel, grid_spec=pltpu.PrefetchScalarGridSpec(num...  17.9 us
    all_to_all x1, blocking collectives, body(): both = lax.all_to_all(part, 'core', 0, 0, tiled=True)  9.18 us

profile of v1, /device:TPU:1, one launch (start us, length us, event | category | flops | bytes accessed | tf_op | source)
XLA Modules:
  0.0 168.8 jit_solution(5400194386476312929)
XLA Ops:
  0.0 0.8 dynamic-slice_convert_fusion
  0.8 1.0 broadcast_multiply_fusion
  1.8 0.7 reshape.31
  2.5 0.7 copy.10
  3.2 0.7 broadcast_in_dim.4
  3.8 0.1 broadcast_in_dim.10
  3.9 31.9 %all_to_all.15 = bf16[64,32,128]{2,1,0:T(8,128)(2,1)S(1)} all-to-all(bf16[64,32,128]{2,1,0:T(8,128)(2,1)S(1)} %bitcast.23), channel_id=1, replica_groups=mesh['x'=4,'y'=8,'z'=8,'core'=2] {'x','z','core'}, dimensions={0} | all-to-all | bytes 1048576 | tf_op jit(solution)/shard_map/all_to_all | solution.py:69
  35.8 0.7 fusion
  37.2 0.1 fusion.1
  37.4 0.1 concatenate.3
  37.5 45.1 %all-gather.2 = f16[16512,128]{1,0:T(8,128)(2,1)S(1)} all-gather(f16[2064,128]{1,0:T(8,128)(2,1)S(1)} %concatenate.3), channel_id=2, replica_groups=mesh['x'=4,'y'=8,'z'=8,'core'=2] {'y'}, dimensions={0}, use_global_device_ids=true | all-gather | bytes 4755456 | tf_op jit(solution)/shard_map/all_gather | solution.py:75
  82.6 0.1 fusion.2
  82.7 2.7 %slice_convert_fusion = bf16[8,2048,128]{2,1,0:T(8,128)(2,1)} fusion(f16[8,2064,128]{2,1,0:T(8,128)(2,1)S(1)} %bitcast.18), kind=kLoop, calls=%fused_computation | loop fusion | flops 2097152 | bytes 8388608 | tf_op jit(solution)/shard_map/convert_element_type | solution.py:77
  85.5 0.5 compare_select_fusion.12.inverse_ref
  86.0 17.9 %shard_map.37 = f32[2,4,2,2,32,1024]{5,4,3,2,1,0:T(8,128)} custom-call(f32[8]{0:T(128)} %compare_select_fusion.12.inverse_ref, bf16[8,4,16,32,128]{4,3,2,1,0:T(8,128)(2,1)} %bitcast.20, bf16[128,4,16,256]{3,2,1,0:T(8,128)(2,1)} %t_ref.1), custom_call_target="tpu_custom_call" | custom-call | flops 4294967296 | bytes 12582912 | tf_op jit(solution)/shard_map/pallas_call | solution.py:43
  103.9 9.2 %all_to_all.16 = f32[2,512,1024]{2,1,0:T(8,128)S(1)} all-to-all(f32[2,512,1024]{2,1,0:T(8,128)} %bitcast.21), channel_id=1, replica_groups=mesh['x'=4,'y'=8,'z'=8,'core'=2] {'core'}, dimensions={0} | all-to-all | bytes 8388608 | tf_op jit(solution)/shard_map/all_to_all | solution.py:79
  113.1 0.5 slice_add_fusion
  113.6 54.2 %all_to_all.17 = f32[8,64,1024]{2,1,0:T(8,128)S(1)} all-to-all(f32[8,64,1024]{2,1,0:T(8,128)S(1)} %bitcast.19), channel_id=1, replica_groups=mesh['x'=4,'y'=8,'z'=8,'core'=2] {'z'}, dimensions={0} | all-to-all | bytes 4194304 | tf_op jit(solution)/shard_map/all_to_all | solution.py:81
  167.9 0.1 reduce_sum.9
  168.0 0.1 convert_element_type.42
  168.1 0.7 copy.11

commit v2 on v1

v2 whole, which is shorter than its diff:
```python
import jax
import jax.numpy as jnp
from jax import lax
from jax.experimental import pallas as pl
from jax.experimental.pallas import tpu as pltpu
from jax.sharding import Mesh, PartitionSpec as P

BF16, F16, F32, I16, I32 = jnp.bfloat16, jnp.float16, jnp.float32, jnp.int16, jnp.int32
LADDER = (64, 32, 16, 8, 4, 2, 1)
X, Y, Z = 4, 8, 8
CHUNKS = ((0, 4),)
FULL = 2.0**14 * 1.875


def raise_to_range(peak):
    peak = jnp.maximum(peak, 2.0**-100)
    scale, power = jnp.ones_like(peak), jnp.zeros_like(peak)
    for step in LADDER:
        fits = peak * scale <= 2.0 ** (15 - step)
        scale = jnp.where(fits, scale * 2.0**step, scale)
        power = jnp.where(fits, power + step, power)
    return scale, power


def lower_again(power):
    scale, left = jnp.ones_like(power), power
    for step in LADDER:
        take = left >= step
        scale = jnp.where(take, scale * 2.0**-step, scale)
        left = jnp.where(take, left - step, left)
    return scale


def code_kernel(own_ref, other_ref, out_ref):
    blocks = own_ref.shape[2] // 128
    for z in range(own_ref.shape[0]):
        value = own_ref[z] + other_ref[z]
        peak = jnp.max(jnp.abs(value), axis=0, keepdims=True)
        power = jnp.floor(jnp.log2(jnp.maximum(peak, 2.0**-100))) + 1.0
        code = jnp.round(value * (jnp.exp2(-power) * FULL)).astype(I32).astype(I16)
        for n in range(blocks):
            out_ref[z, n * 64 : (n + 1) * 64] = code[:, n * 128 : (n + 1) * 128]
        powers = [power[:, n * 128 : (n + 1) * 128] for n in range(blocks)]
        powers = jnp.concatenate(powers + [jnp.zeros((16 - blocks, 128), F32)], axis=0)
        out_ref[z, blocks * 64 :] = powers.astype(I32).astype(I16)


def code_sums(own, other):
    columns = own.shape[2]
    rows = columns // 2 + 16
    spec = pl.BlockSpec((2, 64, columns), lambda z: (z, 0, 0))
    return pl.pallas_call(
        code_kernel,
        grid=(4,),
        in_specs=[spec, spec],
        out_specs=pl.BlockSpec((2, rows, 128), lambda z: (z, 0, 0)),
        out_shape=jax.ShapeDtypeStruct((Z, rows, 128), I16),
        cost_estimate=pl.CostEstimate(
            flops=12 * 512 * columns, bytes_accessed=10 * 512 * columns, transcendentals=0
        ),
    )(own, other)


def total_kernel(*refs):
    out_ref = refs[-1]
    for (first, last), ref in zip(CHUNKS, refs[:-1]):
        blocks = 2 * (last - first)
        powers = [ref[z, 64 * blocks :].astype(I32).astype(F32) for z in range(Z)]
        factors = [jnp.exp2(power) * (1.0 / FULL) for power in powers]
        for n in range(blocks):
            total = None
            for z in range(Z):
                code = ref[z, n * 64 : (n + 1) * 64].astype(I32).astype(F32)
                term = code * factors[z][n : n + 1]
                total = term if total is None else total + term
            total = total.reshape(2, 4, 8, 128)
            for i in range(4):
                both = jnp.concatenate([total[0, i], total[1, i]], axis=0)
                half = pl.ds((n % 2) * 128, 128)
                out_ref[i, first + n // 2, :, half] = both.astype(BF16)


def add_up(shares):
    return pl.pallas_call(
        total_kernel, out_shape=jax.ShapeDtypeStruct((4, 4, 16, 256), BF16)
    )(*shares)


def body(amplitudes, integrals, pair_local):
    core = lax.axis_index("core")
    group = lax.axis_index(("z", "core"))
    weights = lax.dynamic_slice_in_dim(pair_local, group * 8, 8, 1)
    masked = integrals * weights.astype(BF16)[:, :, None, None]
    pieces = masked.reshape(4, 8, 8, 16, 16).transpose(3, 0, 2, 1, 4).reshape(16, 32, 128)
    pieces = jnp.broadcast_to(pieces[None], (X, 16, 32, 128)).reshape(64, 32, 128)
    block = lax.all_to_all(pieces, ("x", "z", "core"), 0, 0, tiled=True)
    columns = amplitudes.reshape(16, 8, 4, 16, 256).transpose(2, 0, 1, 3, 4)
    columns = columns.reshape(4, 16, 128, 256)
    block = block.reshape(2048, 128).astype(F32)
    scale, power = raise_to_range(jnp.max(jnp.abs(block)))
    tail = jnp.broadcast_to(power.astype(F16), (16, 128))
    sent = jnp.concatenate([(block * scale).astype(F16), tail])
    received = lax.all_gather(sent, "y", axis=0)
    inverse = lower_again(received[:, -16, 0].astype(F32)).reshape(2, 2, 2)
    w = received[:, :-16].reshape(2, 2, 2, X, 16, 32, 128)
    targets = (1 - core, core)
    halves = [lax.dynamic_index_in_dim(w, c, 1, keepdims=False) for c in targets]
    scales = [lax.dynamic_index_in_dim(inverse, c, 1, keepdims=False) for c in targets]

    def sums(side, j):
        half, scale = halves[side].astype(BF16), scales[side][None, :, :, None, None]
        part = jnp.einsum("psxgrl,glb->xpsrb", half, columns[j], preferred_element_type=F32)
        return (part * scale).reshape(Z, 64, 256)

    shares = []
    for first, last in CHUNKS:
        other, own = (
            jnp.concatenate([sums(side, j) for j in range(first, last)], axis=-1)
            for side in range(2)
        )
        other = lax.ppermute(other, "core", ((0, 1), (1, 0)))
        coded = code_sums(own, other)
        shares.append(lax.all_to_all(coded, "z", 0, 0, tiled=True))
    return add_up(shares)


def solution(mesh):
    chips = Mesh(mesh.devices.reshape(X, Y, Z, 2), ("x", "y", "z", "core"))
    wide, grp = ("x", "y"), ("z", "core")
    in_specs = (P(None, wide, grp, None), P(None, grp, wide, None), P())
    out_specs = P(None, wide, grp, None)
    return jax.shard_map(body, mesh=chips, in_specs=in_specs, out_specs=out_specs, check_vma=False)
```

time: 169 us -> 143 us (0.85)
  blocking collectives: 140 us -> 78.9 us
  starting transfers between devices: 0 us -> 17.8 us
  local copies, waits for them, and re-layouts: 2.99 us -> 17.5 us
  Pallas kernels: 17.9 us -> 6.34 us
  waiting for transfers between devices: 0 us -> 8.6 us
  matrix products: 0 us -> 7.71 us
  other arithmetic: 6.65 us -> 4.65 us
    all_to_all x3 -> x1, blocking collectives: 95.3 us -> 33.8 us  [body(): shares.append(lax.all_to_all(coded, 'z', 0, 0, tiled=True))]
    all_to_all x0 -> x1, starting transfers between devices: none -> 14.8 us  [body(): block = lax.all_to_all(pieces, ('x', 'z', 'core'), 0, 0, tiled=True)]
    pallas_call x1 -> x2, Pallas kernels: 17.9 us -> 6.34 us  [the longest x1 4.15 us: code_sums(): pl.pallas_call(code_kernel, grid=(4,), in_specs=[spec, spec], out_specs=p...]
    all_to_all x0 -> x1, waiting for transfers between devices: none -> 8.6 us  [body(): block = lax.all_to_all(pieces, ('x', 'z', 'core'), 0, 0, tiled=True)]
    dot_general x0 -> x8, matrix products: none -> 7.71 us  [sums(): jnp.einsum('psxgrl,glb->xpsrb', half, columns[j], preferred_element_type=...]
    slice x0 -> x2, local copies, waits for them, and re-layouts: none -> 6.69 us  [the longest x1 3.93 us: sums(): columns[j]]
    reshape x0 -> x1, local copies, waits for them, and re-layouts: none -> 4.75 us  [body(): columns = amplitudes.reshape(16, 8, 4, 16, 256).transpose(2, 0, 1, 3, 4)]
    ppermute x0 -> x1, starting transfers between devices: none -> 2.98 us  [body(): other = lax.ppermute(other, 'core', ((0, 1), (1, 0)))]
  transfers between devices with their start and end apart: 0 -> 2, of which waited for: 0 -> 1; matrix products, arithmetic and copies ran while one was open for 0% -> 9% of each run, Pallas kernels for 0% -> 0%
where the time goes in v2:
time: 143 us; the launch traced here: 142 us
  blocking collectives  78.9 us (55%)
  starting transfers between devices  17.8 us (12%)
  local copies, waits for them, and re-layouts  17.5 us (12%)
  waiting for transfers between devices  8.6 us (6%)
  matrix products  7.71 us (5%)
  Pallas kernels  6.34 us (4%)
  other arithmetic  4.65 us (3%)
    all_gather x1, blocking collectives, body(): received = lax.all_gather(sent, 'y', axis=0)  45.1 us
    all_to_all x1, blocking collectives, body(): shares.append(lax.all_to_all(coded, 'z', 0, 0, tiled=True))  33.8 us
    all_to_all x1, starting transfers between devices, body(): block = lax.all_to_all(pieces, ('x', 'z', 'core'), 0, 0, tiled=True)  14.8 us
    all_to_all x1, waiting for transfers between devices, body(): block = lax.all_to_all(pieces, ('x', 'z', 'core'), 0, 0, tiled=True)  8.6 us
    dot_general x8, matrix products, sums(): jnp.einsum('psxgrl,glb->xpsrb', half, columns[j], preferred_element_type=...  7.71 us
    reshape x1, local copies, waits for them, and re-layouts, body(): columns = amplitudes.reshape(16, 8, 4, 16, 256).transpose(2, 0, 1, 3, 4)  4.75 us
    pallas_call x1, Pallas kernels, code_sums(): pl.pallas_call(code_kernel, grid=(4,), in_specs=[spec, spec], out_specs=p...  4.15 us
    slice x1, local copies, waits for them, and re-layouts, sums(): columns[j]  3.93 us
  transfers between devices with their start and end apart: 2, of which 1 were waited for; matrix products, arithmetic and copies ran while one was open for 9% of the time, Pallas kernels for 0%

profile of v2, /device:TPU:1, one launch (start us, length us, event | category | flops | bytes accessed | tf_op | source)
XLA Modules:
  0.0 142.4 jit_solution(8823570466983394313)
XLA Ops:
  0.0 0.8 dynamic-slice_convert_fusion
  0.8 1.0 broadcast_multiply_fusion
  1.8 0.7 reshape.68
  2.5 0.7 copy.54
  3.2 0.7 broadcast_in_dim.4
  3.8 0.9 broadcast_in_dim.5
  4.7 14.8 %all-to-all-start = ((bf16[64,32,128]{2,1,0:T(8,128)(2,1)}), bf16[64,32,128]{2,1,0:T(8,128)(2,1)S(1)}, u32[]{:S(2)}, u32[]{:S(2)}) async-start(bf16[64,32,128]{2,1,0:T(8,128)(2,1)} %bitcast.1), calls=%async_computation | async-start | bytes 1048576 | tf_op jit(solution)/shard_map/all_to_all | solution.py:96
  19.5 4.8 %copy.53 = bf16[16,8,4,16,256]{4,3,1,0,2:T(8,128)(2,1)} copy(bf16[16,8,4,16,256]{4,3,2,1,0:T(8,128)(2,1)} %bitcast.252) | data formatting | bytes 8388608 | tf_op jit(solution)/shard_map/reshape | solution.py:97
  24.3 3.9 %fusion.109 = (bf16[1,16,8,16,256]{4,3,2,1,0:T(8,128)(2,1)}, bf16[1,16,8,16,256]{4,3,2,1,0:T(8,128)(2,1)S(1)}, bf16[1,16,8,16,256]{4,3,2,1,0:T(8,128)(2,1)S(1)}, bf16[1,16,8,16,256]{4,3,2,1,0:T(8,128)(2,1)}) fusion(bf16[4,16,8,16,256]{4,3,2,1,0:T(8,128)(2,1)} %bitcast.251), kind=kLoop, calls=%fused_computation.79 | loop fusion | bytes 8388608 | tf_op jit(solution)/shard_map/slice | solution.py:112
  28.2 0.0 copy-start.2
  28.2 8.6 %all-to-all-done = bf16[64,32,128]{2,1,0:T(8,128)(2,1)S(1)} async-done(((bf16[64,32,128]{2,1,0:T(8,128)(2,1)}), bf16[64,32,128]{2,1,0:T(8,128)(2,1)S(1)}, u32[]{:S(2)}, u32[]{:S(2)}) %all-to-all-start) | async-done | bytes 524320 | tf_op jit(solution)/shard_map/all_to_all | solution.py:96
  36.8 0.7 fusion.98
  38.2 0.1 fusion.99
  38.4 0.1 concatenate.9
  38.5 45.1 %all-gather.2 = f16[16512,128]{1,0:T(8,128)(2,1)S(1)} all-gather(f16[2064,128]{1,0:T(8,128)(2,1)S(1)} %concatenate.9), channel_id=2, replica_groups=mesh['x'=4,'y'=8,'z'=8,'core'=2] {'y'}, dimensions={0}, use_global_device_ids=true | all-gather | bytes 4755456 | tf_op jit(solution)/shard_map/all_gather | solution.py:103
  83.6 0.0 copy-start.4
  83.6 2.8 %slice.32 = f16[8,2048,128]{2,1,0:T(8,128)(2,1)} slice(f16[8,2064,128]{2,1,0:T(8,128)(2,1)S(1)} %bitcast.249), slice={[0:8], [0:2048], [0:128]} | slice | bytes 8388608 | tf_op jit(solution)/shard_map/slice | solution.py:105
  86.3 0.1 fusion.100
  86.5 0.1 reshape.80
  86.6 0.0 copy-start
  86.6 2.7 %fusion.68 = f32[4,2,2,32,256]{4,3,0,2,1:T(8,128)S(1)} fusion(bf16[16,128,256,1,1,1]{2,1,0,5,4,3:T(8,128)(2,1)} %bitcast.277, f16[2,2,2,4,16,32,128]{6,5,4,3,2,1,0:T(8,128)(2,1)} %bitcast.253, s32[]{:T(128)S(6)} %select_n.138, f32[2,2]{1,0:T(2,128)S(1)} %bitcast.283), kind=kOutput, calls=%fused_computation.39 | convolution fusion | flops 538050560 | bytes 3670036 | tf_op jit(solution)/shard_map/psxgrl,glb->xpsrb/dot_general | solution.py:112
  89.4 0.0 copy-done.4
  89.4 0.3 copy-done
  89.7 0.7 fusion.77
  90.5 0.0 copy-done.2
  90.5 0.7 fusion.86
  91.3 0.7 fusion.95
  92.0 0.0 copy-start.6
  92.1 0.3 pad_maximum_fusion.1
  92.4 3.0 %collective-permute-start = (f32[8,64,1024]{2,1,0:T(8,128)S(1)}, f32[8,64,1024]{2,1,0:T(8,128)S(1)}, u32[]{:S(2)}, u32[]{:S(2)}) collective-permute-start(f32[8,64,1024]{2,1,0:T(8,128)S(1)} %pad_maximum_fusion.1), channel_id=1, source_target_pairs={{0,1},{1,0},{2,3},{3,2},{4,5},{5,4},{6,7},{7,6},{8,9},{9,8},{10,11... | collective-permute-start | bytes 6291464 | tf_op jit(solution)/shard_map/ppermute | solution.py:121
  95.3 0.0 copy-done.6
  95.4 0.0 copy-start.5
  95.4 0.7 fusion.32
  96.1 0.5 copy-done.5
  96.6 0.0 copy-start.3
  96.6 0.7 fusion.41
  97.3 0.5 copy-done.3
  97.8 0.7 fusion.50
  98.6 0.7 fusion.59
  99.3 1.6 %pad_maximum_fusion.own_ref = f32[8,64,1024]{2,1,0:T(8,128)} fusion(f32[8,64,256]{2,1,0:T(8,128)S(1)} %bitcast.270, f32[8,64,256]{2,1,0:T(8,128)S(1)} %bitcast.267, f32[8,64,256]{2,1,0:T(8,128)S(1)} %bitcast.265, f32[8,64,256]{2,1,0:T(8,128)S(1)} %bitcast.263), kind=kLoop, calls=%fused_computation.1 | loop fusion | flops 1572864 | bytes 4194304 | tf_op jit(solution)/shard_map/concatenate | solution.py:118
  101.0 0.0 collective-permute-done.other_ref
  101.0 0.0 copy-start.1
  101.0 1.3 copy-done.1
  102.3 4.2 %shard_map.37 = s16[8,528,128]{2,1,0:T(8,128)(2,1)} custom-call(f32[8,64,1024]{2,1,0:T(8,128)} %pad_maximum_fusion.own_ref, f32[8,64,1024]{2,1,0:T(8,128)} %copy-done.1), custom_call_target="tpu_custom_call" | custom-call | flops 6291456 | bytes 5242880 | tf_op jit(solution)/shard_map/pallas_call | solution.py:52
  106.4 33.8 %all_to_all.10.refs_0_ = s16[8,528,128]{2,1,0:T(8,128)(2,1)} all-to-all(s16[8,528,128]{2,1,0:T(8,128)(2,1)} %shard_map.37), channel_id=1, replica_groups=mesh['x'=4,'y'=8,'z'=8,'core'=2] {'z'}, dimensions={0} | all-to-all | bytes 2162688 | tf_op jit(solution)/shard_map/all_to_all | solution.py:123
  140.2 2.2 %shard_map.38 = bf16[4,4,16,256]{3,2,1,0:T(8,128)(2,1)} custom-call(s16[8,528,128]{2,1,0:T(8,128)(2,1)} %all_to_all.10.refs_0_), custom_call_target="tpu_custom_call" | custom-call | tf_op jit(solution)/shard_map/pallas_call | solution.py:84
  (10 shorter events, 0.3 us)
Async XLA Ops:
  4.7 32.1 %all-to-all-start = ((bf16[64,32,128]{2,1,0:T(8,128)(2,1)}), bf16[64,32,128]{2,1,0:T(8,128)(2,1)S(1)}, u32[]{:S(2)}, u32[]{:S(2)}) async-start(bf16[64,32,128]{2,1,0:T(8,128)(2,1)} %bitcast.1), calls=%async_computation | async-start | bytes 1048576 | tf_op jit(solution)/shard_map/all_to_all | solution.py:96
  28.2 62.3 %copy-start.2 = (bf16[1,16,8,16,256]{4,3,2,1,0:T(8,128)(2,1)}, bf16[1,16,8,16,256]{4,3,2,1,0:T(8,128)(2,1)S(1)}, u32[]{:S(2)}) copy-start(bf16[1,16,8,16,256]{4,3,2,1,0:T(8,128)(2,1)S(1)} %get-tuple-element.7) | copy-start | bytes 3145732
  83.6 5.8 %copy-start.4 = (bf16[1,16,8,16,256]{4,3,2,1,0:T(8,128)(2,1)S(1)}, bf16[1,16,8,16,256]{4,3,2,1,0:T(8,128)(2,1)}, u32[]{:S(2)}) copy-start(bf16[1,16,8,16,256]{4,3,2,1,0:T(8,128)(2,1)} %get-tuple-element.8) | copy-start | bytes 3145732
  86.6 3.1 %copy-start = (f16[8,2048,128]{2,1,0:T(8,128)(2,1)S(1)}, f16[8,2048,128]{2,1,0:T(8,128)(2,1)}, u32[]{:S(2)}) copy-start(f16[8,2048,128]{2,1,0:T(8,128)(2,1)} %slice.32) | copy-start | bytes 12582916
  92.0 3.3 %copy-start.6 = (bf16[1,16,8,16,256]{4,3,2,1,0:T(8,128)(2,1)S(1)}, bf16[1,16,8,16,256]{4,3,2,1,0:T(8,128)(2,1)}, u32[]{:S(2)}) copy-start(bf16[1,16,8,16,256]{4,3,2,1,0:T(8,128)(2,1)} %get-tuple-element.5) | copy-start | bytes 3145732
  92.4 8.6 %collective-permute-start = (f32[8,64,1024]{2,1,0:T(8,128)S(1)}, f32[8,64,1024]{2,1,0:T(8,128)S(1)}, u32[]{:S(2)}, u32[]{:S(2)}) collective-permute-start(f32[8,64,1024]{2,1,0:T(8,128)S(1)} %pad_maximum_fusion.1), channel_id=1, source_target_pairs={{0,1},{1,0},{2,3},{3,2},{4,5},{5,4},{6,7},{7,6},{8,9},{9,8},{10,11... | collective-permute-start | bytes 6291464 | tf_op jit(solution)/shard_map/ppermute | solution.py:121
  95.4 1.2 copy-start.5
  96.6 1.2 copy-start.3
  101.0 1.3 copy-start.1

commit v3 on v2

v3 whole, which is shorter than its diff:
```python
import jax
import jax.numpy as jnp
from jax import lax
from jax.experimental import pallas as pl
from jax.experimental.pallas import tpu as pltpu
from jax.sharding import Mesh, PartitionSpec as P

BF16, F16, F32, I16, I32 = jnp.bfloat16, jnp.float16, jnp.float32, jnp.int16, jnp.int32
LADDER = (64, 32, 16, 8, 4, 2, 1)
X, Y, Z = 4, 8, 8
FULL = 2.0**14 * 1.875


def raise_to_range(peak):
    peak = jnp.maximum(peak, 2.0**-100)
    scale, power = jnp.ones_like(peak), jnp.zeros_like(peak)
    for step in LADDER:
        fits = peak * scale <= 2.0 ** (15 - step)
        scale = jnp.where(fits, scale * 2.0**step, scale)
        power = jnp.where(fits, power + step, power)
    return scale, power


def lower_again(power):
    scale, left = jnp.ones_like(power), power
    for step in LADDER:
        take = left >= step
        scale = jnp.where(take, scale * 2.0**-step, scale)
        left = jnp.where(take, left - step, left)
    return scale


def cut_kernel(first_ref, pair_ref, in_ref, out_ref):
    lane_block = lax.broadcasted_iota(I32, (8, 128), 1) // 16
    for i in range(4):
        for half in range(2):
            tiles = [
                in_ref[i, k, :, 128 * half : 128 * (half + 1)].astype(F32)
                * pair_ref[i, first_ref[0] + k].astype(F32)
                for k in range(8)
            ]
            for bit in (1, 2, 4):
                low_lanes = (lane_block & bit) == 0
                for k in range(8):
                    if k & bit:
                        continue
                    low, high = tiles[k], tiles[k + bit]
                    tiles[k] = jnp.where(low_lanes, low, pltpu.roll(high, 16 * bit, 1))
                    tiles[k + bit] = jnp.where(
                        low_lanes, pltpu.roll(low, 128 - 16 * bit, 1), high
                    )
            for g in range(8):
                tile = tiles[g].astype(BF16)
                for x in range(X):
                    out_ref[x, 8 * half + g, 8 * i : 8 * (i + 1)] = tile


def cut(first, pair_local, integrals):
    return pl.pallas_call(
        cut_kernel,
        grid_spec=pltpu.PrefetchScalarGridSpec(
            num_scalar_prefetch=2,
            grid=(1,),
            in_specs=[pl.BlockSpec((4, 8, 8, 256), lambda n, f, p: (0, 0, 0, 0))],
            out_specs=pl.BlockSpec((X, 16, 32, 128), lambda n, f, p: (0, 0, 0, 0)),
        ),
        out_shape=jax.ShapeDtypeStruct((X, 16, 32, 128), BF16),
        compiler_params=pltpu.CompilerParams(vmem_limit_bytes=8 << 20),
    )(first, pair_local, integrals)


def code_kernel(own_ref, other_ref, out_ref):
    blocks = own_ref.shape[2] // 128
    for z in range(own_ref.shape[0]):
        value = own_ref[z] + other_ref[z]
        peak = jnp.max(jnp.abs(value), axis=0, keepdims=True)
        power = jnp.floor(jnp.log2(jnp.maximum(peak, 2.0**-100))) + 1.0
        code = jnp.round(value * (jnp.exp2(-power) * FULL)).astype(I32).astype(I16)
        for n in range(blocks):
            out_ref[z, n * 64 : (n + 1) * 64] = code[:, n * 128 : (n + 1) * 128]
        powers = [power[:, n * 128 : (n + 1) * 128] for n in range(blocks)]
        powers = jnp.concatenate(powers + [jnp.zeros((16 - blocks, 128), F32)], axis=0)
        out_ref[z, blocks * 64 :] = powers.astype(I32).astype(I16)


def code_sums(own, other):
    columns = own.shape[2]
    rows = columns // 2 + 16
    spec = pl.BlockSpec((2, 64, columns), lambda z: (z, 0, 0))
    return pl.pallas_call(
        code_kernel,
        grid=(4,),
        in_specs=[spec, spec],
        out_specs=pl.BlockSpec((2, rows, 128), lambda z: (z, 0, 0)),
        out_shape=jax.ShapeDtypeStruct((Z, rows, 128), I16),
        compiler_params=pltpu.CompilerParams(vmem_limit_bytes=12 << 20),
        cost_estimate=pl.CostEstimate(
            flops=12 * 512 * columns, bytes_accessed=10 * 512 * columns, transcendentals=0
        ),
    )(own, other)


def total_kernel(in_ref, out_ref):
    powers = [in_ref[z, 512:].astype(I32).astype(F32) for z in range(Z)]
    factors = [jnp.exp2(power) * (1.0 / FULL) for power in powers]
    for n in range(8):
        total = None
        for z in range(Z):
            code = in_ref[z, n * 64 : (n + 1) * 64].astype(I32).astype(F32)
            term = code * factors[z][n : n + 1]
            total = term if total is None else total + term
        total = total.reshape(2, 4, 8, 128)
        for i in range(4):
            both = jnp.concatenate([total[0, i], total[1, i]], axis=0)
            out_ref[i, n // 2, :, pl.ds((n % 2) * 128, 128)] = both.astype(BF16)


def add_up(shares):
    return pl.pallas_call(
        total_kernel,
        out_shape=jax.ShapeDtypeStruct((4, 4, 16, 256), BF16),
        compiler_params=pltpu.CompilerParams(vmem_limit_bytes=12 << 20),
    )(shares)


def body(amplitudes, integrals, pair_local):
    core = lax.axis_index("core")
    first = 8 * lax.axis_index(("z", "core"))
    pieces = cut(first.reshape(1), pair_local, integrals).reshape(64, 32, 128)
    block = lax.all_to_all(pieces, ("x", "z", "core"), 0, 0, tiled=True)
    columns = amplitudes.reshape(16, 8, 4, 16, 256).transpose(2, 0, 1, 3, 4)
    columns = columns.reshape(4, 16, 128, 256)
    block = block.reshape(2048, 128).astype(F32)
    scale, power = raise_to_range(jnp.max(jnp.abs(block)))
    tail = jnp.broadcast_to(power.astype(F16), (16, 128))
    sent = jnp.concatenate([(block * scale).astype(F16), tail])
    received = lax.all_gather(sent, "y", axis=0)
    inverse = lower_again(received[:, -16, 0].astype(F32)).reshape(2, 2, 2)
    received = received.reshape(2, 2, 2, 2064, 128)
    targets = (1 - core, core)
    scales = [lax.dynamic_index_in_dim(inverse, c, 1, keepdims=False) for c in targets]

    halves = [lax.dynamic_index_in_dim(received, c, 1, keepdims=False) for c in targets]
    halves = lax.optimization_barrier(halves)

    def sums(side, half):
        half = half[:, :, :2048].astype(BF16).reshape(2, 2, X, 16, 32, 128)
        half = lax.optimization_barrier(half)
        scale = scales[side][None, :, :, None, None]
        parts = []
        for j in range(4):
            part = jnp.einsum("psxgrl,glb->xpsrb", half, columns[j], preferred_element_type=F32)
            parts.append((part * scale).reshape(Z, 64, 256))
        return jnp.concatenate(parts, axis=-1)

    other = sums(0, halves[0])
    half, other = lax.optimization_barrier((halves[1], other))
    other = lax.ppermute(other, "core", ((0, 1), (1, 0)))
    coded = code_sums(sums(1, half), other)
    return add_up(lax.all_to_all(coded, "z", 0, 0, tiled=True))


def solution(mesh):
    chips = Mesh(mesh.devices.reshape(X, Y, Z, 2), ("x", "y", "z", "core"))
    wide, grp = ("x", "y"), ("z", "core")
    in_specs = (P(None, wide, grp, None), P(None, grp, wide, None), P())
    out_specs = P(None, wide, grp, None)
    return jax.shard_map(body, mesh=chips, in_specs=in_specs, out_specs=out_specs, check_vma=False)
```

time: 143 us -> 132 us (0.923)
  local copies, waits for them, and re-layouts: 17.5 us -> 12.1 us
  Pallas kernels: 6.34 us -> 3.18 us
    pallas_call x1, Pallas kernels: 4.15 us -> 0.58 us  [code_sums(): pl.pallas_call(code_kernel, grid=(4,), in_specs=[spec, spec], out_specs=p...]
    slice x1 -> x0, local copies, waits for them, and re-layouts: 2.76 us -> none  [body(): w = received[:, :-16].reshape(2, 2, 2, X, 16, 32, 128)]
    pallas_call x0 -> x1, Pallas kernels: none -> 1.66 us  [cut(): pl.pallas_call(cut_kernel, grid_spec=pltpu.PrefetchScalarGridSpec(num_sca...]
    broadcast_in_dim x2 -> x0, local copies, waits for them, and re-layouts: 1.55 us -> none  [body(): jnp.broadcast_to(pieces[None], (X, 16, 32, 128)).reshape(64, 32, 128)]
where the time goes in v3:
time: 132 us
  blocking collectives  77.8 us (59%)
  starting transfers between devices  17.9 us (14%)
  local copies, waits for them, and re-layouts  12.1 us (9%)
  waiting for transfers between devices  8.62 us (7%)
  matrix products  7.71 us (6%)
  other arithmetic  3.62 us (3%)
  Pallas kernels  3.18 us (2%)
    all_gather x1, blocking collectives, body(): received = lax.all_gather(sent, 'y', axis=0)  45.1 us
    all_to_all x1, blocking collectives, body(): return add_up(lax.all_to_all(coded, 'z', 0, 0, tiled=True))  32.7 us
    all_to_all x1, starting transfers between devices, body(): block = lax.all_to_all(pieces, ('x', 'z', 'core'), 0, 0, tiled=True)  14.8 us
    all_to_all x1, waiting for transfers between devices, body(): block = lax.all_to_all(pieces, ('x', 'z', 'core'), 0, 0, tiled=True)  8.59 us
    dot_general x8, matrix products, sums(): jnp.einsum('psxgrl,glb->xpsrb', half, columns[j], preferred_element_type=...  7.71 us
    reshape x1, local copies, waits for them, and re-layouts, body(): columns = amplitudes.reshape(16, 8, 4, 16, 256).transpose(2, 0, 1, 3, 4)  4.75 us
    slice x1, local copies, waits for them, and re-layouts, sums(): columns[j]  3.95 us
    ppermute x1, starting transfers between devices, body(): other = lax.ppermute(other, 'core', ((0, 1), (1, 0)))  3.12 us
  transfers between devices with their start and end apart: 2, of which 1 were waited for; matrix products, arithmetic and copies ran while one was open for 9% of the time, Pallas kernels for 0%

profile of v3, /device:TPU:1, one launch (start us, length us, event | category | flops | bytes accessed | tf_op | source)
XLA Modules:
  0.0 131.9 jit_solution(2378636180682554983)
XLA Ops:
  0.0 0.0 copy-start
  0.0 0.9 copy-done
  0.9 0.0 copy-start.1
  0.9 0.7 copy-done.1
  1.6 1.7 %shard_map.37 = bf16[4,16,32,128]{3,2,1,0:T(8,128)(2,1)} custom-call(s32[1]{0:T(128)} %bitcast.first_ref, s32[4,128]{1,0:T(4,128)S(1)} %copy-done.1, bf16[4,8,8,256]{3,2,1,0:T(8,128)(2,1)S(1)} %copy-done), custom_call_target="tpu_custom_call" | custom-call | tf_op jit(solution)/shard_map/pallas_call | solution.py:59
  3.2 14.8 %all-to-all-start = ((bf16[64,32,128]{2,1,0:T(8,128)(2,1)}), bf16[64,32,128]{2,1,0:T(8,128)(2,1)S(1)}, u32[]{:S(2)}, u32[]{:S(2)}) async-start(bf16[64,32,128]{2,1,0:T(8,128)(2,1)} %bitcast.1), calls=%async_computation | async-start | bytes 1048576 | tf_op jit(solution)/shard_map/all_to_all | solution.py:130
  18.1 4.8 %copy.46 = bf16[16,8,4,16,256]{4,3,1,0,2:T(8,128)(2,1)} copy(bf16[16,8,4,16,256]{4,3,2,1,0:T(8,128)(2,1)} %bitcast.136) | data formatting | bytes 8388608 | tf_op jit(solution)/shard_map/reshape | solution.py:131
  22.8 3.9 %fusion.19 = (bf16[1,16,8,16,256]{4,3,2,1,0:T(8,128)(2,1)}, bf16[1,16,8,16,256]{4,3,2,1,0:T(8,128)(2,1)S(1)}, bf16[1,16,8,16,256]{4,3,2,1,0:T(8,128)(2,1)}, bf16[1,16,8,16,256]{4,3,2,1,0:T(8,128)(2,1)}) fusion(bf16[4,16,8,16,256]{4,3,2,1,0:T(8,128)(2,1)} %bitcast.135), kind=kLoop, calls=%fused_computation.52 | loop fusion | bytes 8388608 | tf_op jit(solution)/shard_map/slice | solution.py:152
  26.8 8.6 %all-to-all-done = bf16[64,32,128]{2,1,0:T(8,128)(2,1)S(1)} async-done(((bf16[64,32,128]{2,1,0:T(8,128)(2,1)}), bf16[64,32,128]{2,1,0:T(8,128)(2,1)S(1)}, u32[]{:S(2)}, u32[]{:S(2)}) %all-to-all-start) | async-done | bytes 524320 | tf_op jit(solution)/shard_map/all_to_all | solution.py:130
  35.4 0.7 fusion.16
  36.7 0.1 fusion.17
  36.9 0.1 concatenate.9
  37.0 45.1 %all-gather.2 = f16[16512,128]{1,0:T(8,128)(2,1)S(1)} all-gather(f16[2064,128]{1,0:T(8,128)(2,1)S(1)} %concatenate.9), channel_id=2, replica_groups=mesh['x'=4,'y'=8,'z'=8,'core'=2] {'y'}, dimensions={0}, use_global_device_ids=true | all-gather | bytes 4755456 | tf_op jit(solution)/shard_map/all_gather | solution.py:137
  82.1 0.8 dynamic-slice_bitcast_fusion
  82.9 1.7 %slice_convert_fusion.1 = bf16[2,2,2048,128]{3,2,1,0:T(8,128)(2,1)} fusion(f16[2,2,2064,128]{3,2,1,0:T(8,128)(2,1)S(1)} %get-tuple-element.10), kind=kLoop, calls=%fused_computation.6 | loop fusion | flops 1048576 | bytes 4194304 | tf_op jit(solution)/shard_map/convert_element_type | solution.py:147
  84.6 0.1 fusion.18
  84.8 0.1 reshape.78
  84.9 0.0 copy-start.2
  84.9 0.0 copy-start.4
  84.9 2.7 %fusion.1 = f32[4,2,2,32,256]{4,3,0,2,1:T(8,128)S(1)} fusion(bf16[2,2,4,16,32,128]{5,4,3,2,1,0:T(8,128)(2,1)} %bitcast.137, bf16[16,128,256,1,1,1]{2,1,0,5,4,3:T(8,128)(2,1)} %bitcast.160, f32[2,2]{1,0:T(2,128)S(1)} %bitcast.166), kind=kOutput, calls=%fused_computation.18 | convolution fusion | flops 537001984 | bytes 3670032 | tf_op jit(solution)/shard_map/psxgrl,glb->xpsrb/dot_general | solution.py:152
  87.7 0.0 copy-done.2
  87.7 0.0 copy-done.4
  87.7 0.0 copy-start.3
  87.7 0.7 fusion.3
  88.5 0.4 copy-done.3
  88.9 0.7 fusion.5
  89.7 0.7 fusion.7
  90.5 0.3 pad_maximum_fusion
  90.8 0.0 copy-start.5
  90.8 3.1 %collective-permute-start = (f32[8,64,1024]{2,1,0:T(8,128)S(1)}, f32[8,64,1024]{2,1,0:T(8,128)S(1)}, u32[]{:S(2)}, u32[]{:S(2)}) collective-permute-start(f32[8,64,1024]{2,1,0:T(8,128)S(1)} %pad_maximum_fusion), channel_id=1, source_target_pairs={{0,1},{1,0},{2,3},{3,2},{4,5},{5,4},{6,7},{7,6},{8,9},{9,8},{10,11... | collective-permute-start | bytes 6291464 | tf_op jit(solution)/shard_map/ppermute | solution.py:158
  93.9 0.4 slice_convert_fusion
  94.3 0.0 copy-done.5
  94.3 0.7 fusion.9
  95.0 0.7 fusion.11
  95.8 0.7 fusion.13
  96.6 0.7 fusion.15
  97.4 0.3 pad_maximum_fusion.1.own_ref
  97.6 0.0 collective-permute-done.other_ref
  97.7 0.6 shard_map.38
  98.3 32.7 %all_to_all.10.in_ref = s16[8,528,128]{2,1,0:T(8,128)(2,1)S(1)} all-to-all(s16[8,528,128]{2,1,0:T(8,128)(2,1)S(1)} %shard_map.38), channel_id=1, replica_groups=mesh['x'=4,'y'=8,'z'=8,'core'=2] {'z'}, dimensions={0} | all-to-all | bytes 2162688 | tf_op jit(solution)/shard_map/all_to_all | solution.py:160
  131.0 0.9 shard_map.39
  (10 shorter events, 0.3 us)
Async XLA Ops:
  0.0 0.9 copy-start
  0.9 0.7 copy-start.1
  3.2 32.1 %all-to-all-start = ((bf16[64,32,128]{2,1,0:T(8,128)(2,1)}), bf16[64,32,128]{2,1,0:T(8,128)(2,1)S(1)}, u32[]{:S(2)}, u32[]{:S(2)}) async-start(bf16[64,32,128]{2,1,0:T(8,128)(2,1)} %bitcast.1), calls=%async_computation | async-start | bytes 1048576 | tf_op jit(solution)/shard_map/all_to_all | solution.py:130
  84.9 2.8 %copy-start.2 = (bf16[2,2,2048,128]{3,2,1,0:T(8,128)(2,1)S(1)}, bf16[2,2,2048,128]{3,2,1,0:T(8,128)(2,1)}, u32[]{:S(2)}) copy-start(bf16[2,2,2048,128]{3,2,1,0:T(8,128)(2,1)} %slice_convert_fusion.1) | copy-start | bytes 6291460
  84.9 2.8 %copy-start.4 = (bf16[1,16,8,16,256]{4,3,2,1,0:T(8,128)(2,1)S(1)}, bf16[1,16,8,16,256]{4,3,2,1,0:T(8,128)(2,1)}, u32[]{:S(2)}) copy-start(bf16[1,16,8,16,256]{4,3,2,1,0:T(8,128)(2,1)} %get-tuple-element.18) | copy-start | bytes 3145732
  87.7 1.2 copy-start.3
  90.8 3.5 %copy-start.5 = (bf16[1,16,8,16,256]{4,3,2,1,0:T(8,128)(2,1)S(1)}, bf16[1,16,8,16,256]{4,3,2,1,0:T(8,128)(2,1)}, u32[]{:S(2)}) copy-start(bf16[1,16,8,16,256]{4,3,2,1,0:T(8,128)(2,1)} %get-tuple-element.15) | copy-start | bytes 3145732
  90.8 6.9 %collective-permute-start = (f32[8,64,1024]{2,1,0:T(8,128)S(1)}, f32[8,64,1024]{2,1,0:T(8,128)S(1)}, u32[]{:S(2)}, u32[]{:S(2)}) collective-permute-start(f32[8,64,1024]{2,1,0:T(8,128)S(1)} %pad_maximum_fusion), channel_id=1, source_target_pairs={{0,1},{1,0},{2,3},{3,2},{4,5},{5,4},{6,7},{7,6},{8,9},{9,8},{10,11... | collective-permute-start | bytes 6291464 | tf_op jit(solution)/shard_map/ppermute | solution.py:158

commit v4 on v3

--- a/solution.py
+++ b/solution.py
@@ -65,7 +65,6 @@
             out_specs=pl.BlockSpec((X, 16, 32, 128), lambda n, f, p: (0, 0, 0, 0)),
         ),
         out_shape=jax.ShapeDtypeStruct((X, 16, 32, 128), BF16),
-        compiler_params=pltpu.CompilerParams(vmem_limit_bytes=8 << 20),
     )(first, pair_local, integrals)
 
 
@@ -135,28 +134,24 @@
     tail = jnp.broadcast_to(power.astype(F16), (16, 128))
     sent = jnp.concatenate([(block * scale).astype(F16), tail])
     received = lax.all_gather(sent, "y", axis=0)
-    inverse = lower_again(received[:, -16, 0].astype(F32)).reshape(2, 2, 2)
     received = received.reshape(2, 2, 2, 2064, 128)
     targets = (1 - core, core)
-    scales = [lax.dynamic_index_in_dim(inverse, c, 1, keepdims=False) for c in targets]
-
     halves = [lax.dynamic_index_in_dim(received, c, 1, keepdims=False) for c in targets]
     halves = lax.optimization_barrier(halves)
 
-    def sums(side, half):
-        half = half[:, :, :2048].astype(BF16).reshape(2, 2, X, 16, 32, 128)
-        half = lax.optimization_barrier(half)
-        scale = scales[side][None, :, :, None, None]
+    def sums(side, cuts):
+        scale = lower_again(halves[side][:, :, 2048, 0].astype(F32))[None, :, :, None, None]
         parts = []
-        for j in range(4):
-            part = jnp.einsum("psxgrl,glb->xpsrb", half, columns[j], preferred_element_type=F32)
-            parts.append((part * scale).reshape(Z, 64, 256))
+        for cut_columns in cuts:
+            half, *some = lax.optimization_barrier((halves[side], *(columns[j] for j in cut_columns)))
+            half = half[:, :, :2048].astype(BF16).reshape(2, 2, X, 16, 32, 128)
+            for column in some:
+                part = jnp.einsum("psxgrl,glb->xpsrb", half, column, preferred_element_type=F32)
+                parts.append((part * scale).reshape(Z, 64, 256))
         return jnp.concatenate(parts, axis=-1)
 
-    other = sums(0, halves[0])
-    half, other = lax.optimization_barrier((halves[1], other))
-    other = lax.ppermute(other, "core", ((0, 1), (1, 0)))
-    coded = code_sums(sums(1, half), other)
+    other = lax.ppermute(sums(0, ((0,), (1,), (2, 3))), "core", ((0, 1), (1, 0)))
+    coded = code_sums(sums(1, ((0, 1, 2, 3),)), other)
     return add_up(lax.all_to_all(coded, "z", 0, 0, tiled=True))
 
 

time: 132 us -> 130 us (0.985)
  local copies, waits for them, and re-layouts: 12.1 us -> 6.5 us
  waiting for transfers between devices: 8.62 us -> 13.3 us
  matrix products: 7.71 us -> 5.78 us
    reshape x1 -> x0, local copies, waits for them, and re-layouts: 4.75 us -> none  [body(): columns = amplitudes.reshape(16, 8, 4, 16, 256).transpose(2, 0, 1, 3, 4)]
    all_to_all x1, waiting for transfers between devices: 8.59 us -> 13.3 us  [body(): block = lax.all_to_all(pieces, ('x', 'z', 'core'), 0, 0, tiled=True)]
    dot_general x8, matrix products: 7.71 us -> 5.78 us  [sums(): jnp.einsum('psxgrl,glb->xpsrb', half, column, preferred_element_type=F32)]
  transfers between devices with their start and end apart: 2 -> 2, of which waited for: 1 -> 1; matrix products, arithmetic and copies ran while one was open for 9% -> 6% of each run, Pallas kernels for 0% -> 0%
where the time goes in v4:
time: 130 us
  blocking collectives  78 us (60%)
  starting transfers between devices  17.8 us (14%)
  waiting for transfers between devices  13.3 us (10%)
  local copies, waits for them, and re-layouts  6.5 us (5%)
  matrix products  5.78 us (4%)
  Pallas kernels  4.24 us (3%)
  other arithmetic  2.97 us (2%)
    all_gather x1, blocking collectives, body(): received = lax.all_gather(sent, 'y', axis=0)  45.1 us
    all_to_all x1, blocking collectives, body(): return add_up(lax.all_to_all(coded, 'z', 0, 0, tiled=True))  32.9 us
    all_to_all x1, starting transfers between devices, body(): block = lax.all_to_all(pieces, ('x', 'z', 'core'), 0, 0, tiled=True)  14.8 us
    all_to_all x1, waiting for transfers between devices, body(): block = lax.all_to_all(pieces, ('x', 'z', 'core'), 0, 0, tiled=True)  13.3 us
    dot_general x8, matrix products, sums(): jnp.einsum('psxgrl,glb->xpsrb', half, column, preferred_element_type=F32)  5.78 us
    slice x1, local copies, waits for them, and re-layouts, sums(): columns[j]  3.97 us
    ppermute x1, starting transfers between devices, body(): lax.ppermute(sums(0, ((0,), (1,), (2, 3))), 'core', ((0, 1), (1, 0)))  2.99 us
    pallas_call x1, Pallas kernels, cut(): pl.pallas_call(cut_kernel, grid_spec=pltpu.PrefetchScalarGridSpec(num_sca...  2.7 us
  transfers between devices with their start and end apart: 2, of which 1 were waited for; matrix products, arithmetic and copies ran while one was open for 6% of the time, Pallas kernels for 0%

profile of v4, /device:TPU:1, one launch (start us, length us, event | category | flops | bytes accessed | tf_op | source)
XLA Modules:
  0.0 129.6 jit_solution(12686137140905768105)
XLA Ops:
  0.0 2.7 %shard_map.37 = bf16[4,16,32,128]{3,2,1,0:T(8,128)(2,1)} custom-call(s32[1]{0:T(128)} %bitcast.first_ref, s32[4,128]{1,0:T(4,128)} %pair_ref.1, bf16[4,8,8,256]{3,2,1,0:T(8,128)(2,1)} %in_ref.1), custom_call_target="tpu_custom_call" | custom-call | tf_op jit(solution)/shard_map/pallas_call | solution.py:59
  2.7 14.8 %all-to-all-start = ((bf16[64,32,128]{2,1,0:T(8,128)(2,1)}), bf16[64,32,128]{2,1,0:T(8,128)(2,1)S(1)}, u32[]{:S(2)}, u32[]{:S(2)}) async-start(bf16[64,32,128]{2,1,0:T(8,128)(2,1)} %bitcast.157), calls=%async_computation | async-start | bytes 1048576 | tf_op jit(solution)/shard_map/all_to_all | solution.py:129
  17.5 4.0 %fusion.26 = (bf16[1,16,8,16,256]{4,3,0,2,1:T(8,128)(2,1)}, bf16[1,16,8,16,256]{4,3,0,2,1:T(8,128)(2,1)}, bf16[1,16,8,16,256]{4,3,0,2,1:T(8,128)(2,1)S(1)}, bf16[1,16,8,16,256]{4,3,0,2,1:T(8,128)(2,1)S(1)}) fusion(bf16[4,16,8,16,256]{4,3,0,2,1:T(8,128)(2,1)} %bitcast.148), kind=kLoop, calls=%fused_computation.72 | loop fusion | bytes 8388608 | tf_op jit(solution)/shard_map/slice | solution.py:146
  21.5 13.3 %all-to-all-done = bf16[64,32,128]{2,1,0:T(8,128)(2,1)S(1)} async-done(((bf16[64,32,128]{2,1,0:T(8,128)(2,1)}), bf16[64,32,128]{2,1,0:T(8,128)(2,1)S(1)}, u32[]{:S(2)}, u32[]{:S(2)}) %all-to-all-start) | async-done | bytes 524320 | tf_op jit(solution)/shard_map/all_to_all | solution.py:129
  34.8 0.7 fusion.16
  36.2 0.1 fusion.17
  36.3 0.1 concatenate.9
  36.5 45.1 %all-gather.2 = f16[16512,128]{1,0:T(8,128)(2,1)S(1)} all-gather(f16[2064,128]{1,0:T(8,128)(2,1)S(1)} %concatenate.9), channel_id=2, replica_groups=mesh['x'=4,'y'=8,'z'=8,'core'=2] {'y'}, dimensions={0}, use_global_device_ids=true | all-gather | bytes 4755456 | tf_op jit(solution)/shard_map/all_gather | solution.py:136
  81.6 0.8 dynamic-slice_bitcast_fusion
  82.4 0.1 convert_reduce_fusion
  82.5 0.0 copy-start.1
  82.5 0.4 slice_convert_fusion
  82.9 0.8 copy-done.1
  83.7 0.0 copy-start
  83.7 0.7 fusion.15
  84.5 0.5 copy-done
  84.9 0.7 fusion.13
  85.7 0.4 slice_convert_fusion.1
  86.1 0.7 fusion.11
  86.8 0.4 slice_convert_fusion.2
  87.2 0.7 fusion.9
  88.0 0.3 pad_maximum_fusion.1
  88.3 3.0 %collective-permute-start = (f32[8,64,1024]{2,1,0:T(8,128)S(1)}, f32[8,64,1024]{2,1,0:T(8,128)S(1)}, u32[]{:S(2)}, u32[]{:S(2)}) collective-permute-start(f32[8,64,1024]{2,1,0:T(8,128)S(1)} %pad_maximum_fusion.1), channel_id=1, source_target_pairs={{0,1},{1,0},{2,3},{3,2},{4,5},{5,4},{6,7},{7,6},{8,9},{9,8},{10,11... | collective-permute-start | bytes 6291464 | tf_op jit(solution)/shard_map/ppermute | solution.py:153
  91.3 0.4 slice_convert_fusion.3
  91.7 0.7 fusion.7
  92.5 0.7 fusion.5
  93.3 0.7 fusion.3
  94.0 0.7 fusion.1
  94.8 0.3 pad_maximum_fusion.own_ref
  95.1 0.0 collective-permute-done.other_ref
  95.1 0.6 shard_map.38
  95.7 32.9 %all_to_all.10.in_ref = s16[8,528,128]{2,1,0:T(8,128)(2,1)S(1)} all-to-all(s16[8,528,128]{2,1,0:T(8,128)(2,1)S(1)} %shard_map.38), channel_id=1, replica_groups=mesh['x'=4,'y'=8,'z'=8,'core'=2] {'z'}, dimensions={0} | all-to-all | bytes 2162688 | tf_op jit(solution)/shard_map/all_to_all | solution.py:155
  128.7 0.9 shard_map.39
  (10 shorter events, 0.3 us)
Async XLA Ops:
  2.7 32.1 %all-to-all-start = ((bf16[64,32,128]{2,1,0:T(8,128)(2,1)}), bf16[64,32,128]{2,1,0:T(8,128)(2,1)S(1)}, u32[]{:S(2)}, u32[]{:S(2)}) async-start(bf16[64,32,128]{2,1,0:T(8,128)(2,1)} %bitcast.157), calls=%async_computation | async-start | bytes 1048576 | tf_op jit(solution)/shard_map/all_to_all | solution.py:129
  82.5 1.2 copy-start.1
  83.7 1.2 copy-start
  88.3 6.8 %collective-permute-start = (f32[8,64,1024]{2,1,0:T(8,128)S(1)}, f32[8,64,1024]{2,1,0:T(8,128)S(1)}, u32[]{:S(2)}, u32[]{:S(2)}) collective-permute-start(f32[8,64,1024]{2,1,0:T(8,128)S(1)} %pad_maximum_fusion.1), channel_id=1, source_target_pairs={{0,1},{1,0},{2,3},{3,2},{4,5},{5,4},{6,7},{7,6},{8,9},{9,8},{10,11... | collective-permute-start | bytes 6291464 | tf_op jit(solution)/shard_map/ppermute | solution.py:153

commit v5 on v4

--- a/solution.py
+++ b/solution.py
@@ -51,8 +51,7 @@
                     )
             for g in range(8):
                 tile = tiles[g].astype(BF16)
-                for x in range(X):
-                    out_ref[x, 8 * half + g, 8 * i : 8 * (i + 1)] = tile
+                out_ref[8 * half + g, 8 * i : 8 * (i + 1)] = tile
 
 
 def cut(first, pair_local, integrals):
@@ -62,9 +61,9 @@
             num_scalar_prefetch=2,
             grid=(1,),
             in_specs=[pl.BlockSpec((4, 8, 8, 256), lambda n, f, p: (0, 0, 0, 0))],
-            out_specs=pl.BlockSpec((X, 16, 32, 128), lambda n, f, p: (0, 0, 0, 0)),
+            out_specs=pl.BlockSpec((16, 32, 128), lambda n, f, p: (0, 0, 0)),
         ),
-        out_shape=jax.ShapeDtypeStruct((X, 16, 32, 128), BF16),
+        out_shape=jax.ShapeDtypeStruct((16, 32, 128), BF16),
     )(first, pair_local, integrals)
 
 
@@ -125,32 +124,35 @@
 def body(amplitudes, integrals, pair_local):
     core = lax.axis_index("core")
     first = 8 * lax.axis_index(("z", "core"))
-    pieces = cut(first.reshape(1), pair_local, integrals).reshape(64, 32, 128)
-    block = lax.all_to_all(pieces, ("x", "z", "core"), 0, 0, tiled=True)
+    pieces = cut(first.reshape(1), pair_local, integrals)
+    block = lax.all_to_all(pieces, ("z", "core"), 0, 0, tiled=True)
     columns = amplitudes.reshape(16, 8, 4, 16, 256).transpose(2, 0, 1, 3, 4)
     columns = columns.reshape(4, 16, 128, 256)
-    block = block.reshape(2048, 128).astype(F32)
+    block = block.reshape(512, 128).astype(F32)
     scale, power = raise_to_range(jnp.max(jnp.abs(block)))
-    tail = jnp.broadcast_to(power.astype(F16), (16, 128))
+    tail = jnp.broadcast_to(power.astype(F16), (8, 128))
     sent = jnp.concatenate([(block * scale).astype(F16), tail])
-    received = lax.all_gather(sent, "y", axis=0)
-    received = received.reshape(2, 2, 2, 2064, 128)
+    received = lax.all_gather(sent, ("y", "x"), axis=0)
+    received = received.reshape(2, 2, 2, X, 520, 128)
     targets = (1 - core, core)
     halves = [lax.dynamic_index_in_dim(received, c, 1, keepdims=False) for c in targets]
     halves = lax.optimization_barrier(halves)
 
     def sums(side, cuts):
-        scale = lower_again(halves[side][:, :, 2048, 0].astype(F32))[None, :, :, None, None]
-        parts = []
+        scale = lower_again(halves[side][:, :, :, 512, 0].astype(F32)).transpose(2, 0, 1)[..., None, None]
+        parts = {}
         for cut_columns in cuts:
-            half, *some = lax.optimization_barrier((halves[side], *(columns[j] for j in cut_columns)))
-            half = half[:, :, :2048].astype(BF16).reshape(2, 2, X, 16, 32, 128)
-            for column in some:
+            some = [columns[j] for j in cut_columns]
+            earlier = [parts[j] for j in parts]
+            half, some, earlier = lax.optimization_barrier((halves[side], some, earlier))
+            parts = dict(zip(parts, earlier))
+            half = half[:, :, :, :512].astype(BF16).reshape(2, 2, X, 16, 32, 128)
+            for j, column in zip(cut_columns, some):
                 part = jnp.einsum("psxgrl,glb->xpsrb", half, column, preferred_element_type=F32)
-                parts.append((part * scale).reshape(Z, 64, 256))
-        return jnp.concatenate(parts, axis=-1)
+                parts[j] = (part * scale).reshape(Z, 64, 256)
+        return jnp.concatenate([parts[j] for j in range(4)], axis=-1)
 
-    other = lax.ppermute(sums(0, ((0,), (1,), (2, 3))), "core", ((0, 1), (1, 0)))
+    other = lax.ppermute(sums(0, ((2, 3), (0, 1))), "core", ((0, 1), (1, 0)))
     coded = code_sums(sums(1, ((0, 1, 2, 3),)), other)
     return add_up(lax.all_to_all(coded, "z", 0, 0, tiled=True))
 

time: 130 us -> 127 us (0.977)
  waiting for transfers between devices: 13.3 us -> 5.19 us
  starting transfers between devices: 17.8 us -> 24.4 us
    ppermute x1, starting transfers between devices: 2.99 us -> 12.5 us  [body(): other = lax.ppermute(sums(0, ((2, 3), (0, 1))), 'core', ((0, 1), (1, 0)))]
    all_to_all x1, waiting for transfers between devices: 13.3 us -> 5.18 us  [body(): block = lax.all_to_all(pieces, ('z', 'core'), 0, 0, tiled=True)]
    all_to_all x1, starting transfers between devices: 14.8 us -> 11.8 us  [body(): block = lax.all_to_all(pieces, ('z', 'core'), 0, 0, tiled=True)]
where the time goes in v5:
time: 127 us
  blocking collectives  78.1 us (61%)
  starting transfers between devices  24.4 us (19%)
  matrix products  5.79 us (5%)
  local copies, waits for them, and re-layouts  5.29 us (4%)
  waiting for transfers between devices  5.19 us (4%)
  Pallas kernels  4.06 us (3%)
  other arithmetic  2.83 us (2%)
    all_gather x1, blocking collectives, body(): received = lax.all_gather(sent, ('y', 'x'), axis=0)  45.6 us
    all_to_all x1, blocking collectives, body(): return add_up(lax.all_to_all(coded, 'z', 0, 0, tiled=True))  32.5 us
    ppermute x1, starting transfers between devices, body(): other = lax.ppermute(sums(0, ((2, 3), (0, 1))), 'core', ((0, 1), (1, 0)))  12.5 us
    all_to_all x1, starting transfers between devices, body(): block = lax.all_to_all(pieces, ('z', 'core'), 0, 0, tiled=True)  11.8 us
    dot_general x8, matrix products, sums(): jnp.einsum('psxgrl,glb->xpsrb', half, column, preferred_element_type=F32)  5.79 us
    all_to_all x1, waiting for transfers between devices, body(): block = lax.all_to_all(pieces, ('z', 'core'), 0, 0, tiled=True)  5.18 us
    slice x1, local copies, waits for them, and re-layouts, sums(): some = [columns[j] for j in cut_columns]  3.7 us
  transfers between devices with their start and end apart: 2, of which 1 were waited for; matrix products, arithmetic and copies ran while one was open for 6% of the time, Pallas kernels for 0%

profile of v5, /device:TPU:1, one launch (start us, length us, event | category | flops | bytes accessed | tf_op | source)
XLA Modules:
  0.0 126.6 jit_solution(11717778581917578483)
XLA Ops:
  0.0 2.5 %shard_map.37 = bf16[16,32,128]{2,1,0:T(8,128)(2,1)} custom-call(s32[1]{0:T(128)} %bitcast.first_ref, s32[4,128]{1,0:T(4,128)} %pair_ref.1, bf16[4,8,8,256]{3,2,1,0:T(8,128)(2,1)} %in_ref.1), custom_call_target="tpu_custom_call" | custom-call | tf_op jit(solution)/shard_map/pallas_call | solution.py:58
  2.5 11.8 %all-to-all-start = ((bf16[16,32,128]{2,1,0:T(8,128)(2,1)}), bf16[16,32,128]{2,1,0:T(8,128)(2,1)S(1)}, u32[]{:S(2)}, u32[]{:S(2)}) async-start(bf16[16,32,128]{2,1,0:T(8,128)(2,1)} %shard_map.37), calls=%async_computation | async-start | bytes 262144 | tf_op jit(solution)/shard_map/all_to_all | solution.py:128
  14.3 3.7 %fusion.20 = (bf16[1,16,8,16,256]{4,3,0,2,1:T(8,128)(2,1)}, bf16[1,16,8,16,256]{4,3,0,2,1:T(8,128)(2,1)S(1)}, bf16[1,16,8,16,256]{4,3,0,2,1:T(8,128)(2,1)S(1)}, bf16[1,16,8,16,256]{4,3,0,2,1:T(8,128)(2,1)S(1)}) fusion(bf16[4,16,8,16,256]{4,3,0,2,1:T(8,128)(2,1)} %bitcast.138), kind=kLoop, calls=%fused_computation.65 | loop fusion | bytes 8388608 | tf_op jit(solution)/shard_map/slice | solution.py:145
  18.0 5.2 %all-to-all-done = bf16[16,32,128]{2,1,0:T(8,128)(2,1)S(1)} async-done(((bf16[16,32,128]{2,1,0:T(8,128)(2,1)}), bf16[16,32,128]{2,1,0:T(8,128)(2,1)S(1)}, u32[]{:S(2)}, u32[]{:S(2)}) %all-to-all-start) | async-done | bytes 131104 | tf_op jit(solution)/shard_map/all_to_all | solution.py:128
  23.2 0.6 fusion.16
  24.6 45.6 %all-gather.2 = f16[16640,128]{1,0:T(8,128)(2,1)S(1)} all-gather(f16[520,128]{1,0:T(8,128)(2,1)S(1)} %concatenate.9), channel_id=2, replica_groups=mesh['x'=4,'y'=8,'z'=8,'core'=2] {'y','x'}, dimensions={0}, use_global_device_ids=true | all-gather | bytes 4392960 | tf_op jit(solution)/shard_map/all_gather | solution.py:135
  70.2 0.8 dynamic-slice_bitcast_fusion
  71.1 0.1 convert_reduce_fusion
  71.2 0.5 slice_convert_fusion.1
  71.7 0.0 copy-start
  71.7 0.7 fusion.4
  72.5 0.4 copy-done
  72.9 0.7 fusion.5
  73.7 0.5 slice_convert_fusion
  74.2 0.7 fusion.7
  75.0 0.7 fusion.6
  75.7 0.3 pad_maximum_fusion.1
  76.0 12.5 %collective-permute-start = (f32[8,64,1024]{2,1,0:T(8,128)S(1)}, f32[8,64,1024]{2,1,0:T(8,128)S(1)}, u32[]{:S(2)}, u32[]{:S(2)}) collective-permute-start(f32[8,64,1024]{2,1,0:T(8,128)S(1)} %pad_maximum_fusion.1), channel_id=1, source_target_pairs={{0,1},{1,0},{2,3},{3,2},{4,5},{5,4},{6,7},{7,6},{8,9},{9,8},{10,11... | collective-permute-start | bytes 6291464 | tf_op jit(solution)/shard_map/ppermute | solution.py:155
  88.6 0.5 slice_convert_fusion.2
  89.1 0.7 fusion.3
  89.9 0.7 fusion.2
  90.6 0.7 fusion.1
  91.4 0.7 fusion
  92.2 0.3 pad_maximum_fusion.own_ref
  92.5 0.0 collective-permute-done.other_ref
  92.5 0.6 shard_map.38
  93.1 32.5 %all_to_all.10.in_ref = s16[8,528,128]{2,1,0:T(8,128)(2,1)S(1)} all-to-all(s16[8,528,128]{2,1,0:T(8,128)(2,1)S(1)} %shard_map.38), channel_id=1, replica_groups=mesh['x'=4,'y'=8,'z'=8,'core'=2] {'z'}, dimensions={0} | all-to-all | bytes 2162688 | tf_op jit(solution)/shard_map/all_to_all | solution.py:157
  125.6 0.9 shard_map.39
  (12 shorter events, 0.4 us)
Async XLA Ops:
  2.5 20.7 %all-to-all-start = ((bf16[16,32,128]{2,1,0:T(8,128)(2,1)}), bf16[16,32,128]{2,1,0:T(8,128)(2,1)S(1)}, u32[]{:S(2)}, u32[]{:S(2)}) async-start(bf16[16,32,128]{2,1,0:T(8,128)(2,1)} %shard_map.37), calls=%async_computation | async-start | bytes 262144 | tf_op jit(solution)/shard_map/all_to_all | solution.py:128
  71.7 1.2 copy-start
  76.0 16.4 %collective-permute-start = (f32[8,64,1024]{2,1,0:T(8,128)S(1)}, f32[8,64,1024]{2,1,0:T(8,128)S(1)}, u32[]{:S(2)}, u32[]{:S(2)}) collective-permute-start(f32[8,64,1024]{2,1,0:T(8,128)S(1)} %pad_maximum_fusion.1), channel_id=1, source_target_pairs={{0,1},{1,0},{2,3},{3,2},{4,5},{5,4},{6,7},{7,6},{8,9},{9,8},{10,11... | collective-permute-start | bytes 6291464 | tf_op jit(solution)/shard_map/ppermute | solution.py:155
